TPU v7x, 512 devices: a whole 4x4x16 slice. The times are simulated.
512 devices in a mesh: pair: 32 (over y, z_lo), row: 16 (over z_hi, x, core).
Axes of the slice: x: 4, y: 4, z: 16 (z_hi: 2, z_lo: 8; z = z_hi * 8 + z_lo), core: 2. Of those that a mesh axis runs over, the one named last changes fastest.
Arguments:
- factor: float32 [8192, 16384], P('row', 'pair'), may hold values from -6 to 6
- plan: int32 [2, 512], replicated, may hold values from 0 to 511, each once within a row
Outputs:
- rotated: float32 [8192, 16384], P('row', 'pair')
Inputs may be any that keep to these rules, and one draw needn't show every extreme that they name: Each row of plan names every number of 0 to 511 once.
All inputs are finite; a program needn't handle non-finite values.
Results may differ from a plain program's by a relative error of at most 0.0001.
Values sent between devices are 32-bit elements; how exact they have to be, the bound alone decides.
A program may use at most 64 MiB of HBM per device.

v0:
```python
import jax
import jax.numpy as jnp
from jax import lax
from jax.sharding import PartitionSpec as P

BLK = 256
ROUNDS = 2
NS_STEPS = 3
eps_value = 1e-06


def from_behind(value, axis, by):
    devices = lax.axis_size(axis)
    return lax.ppermute(value, axis, [(i, (i + by) % devices) for i in range(devices)])


def product(left, right):
    return jnp.dot(left, right, precision=lax.Precision.HIGHEST, preferred_element_type=jnp.float32)


def sign_table(width, col_ids):
    rows_idx = jnp.arange(width)[:, None]
    cols_idx = col_ids[None, :]
    positive = (rows_idx < BLK) & (cols_idx >= BLK)
    negative = (rows_idx >= BLK) & (cols_idx < BLK)
    sign = jnp.where(positive, 1.0, jnp.where(negative, -1.0, 0.0)).astype(jnp.float32)
    unit = (rows_idx == cols_idx).astype(jnp.float32)
    return (sign, positive, unit)


def shards(factor, plan):
    width = factor.shape[1]
    blocks = factor
    for rnd in range(ROUNDS):
        work = jnp.take(blocks, plan[rnd], axis=1)
        partial_value = product(work.T, work)
        groups = lax.axis_size("row")
        count = width // groups
        half = count // 2
        device = lax.axis_index("row")
        spot = jnp.arange(count)
        own_ids = spot // half * BLK + device * half + spot % half
        mixed = (
            partial_value.reshape(width, 2, groups, half)
            .transpose(0, 2, 1, 3)
            .reshape(width, width)
        )
        columns = lax.psum_scatter(mixed, "row", scatter_dimension=1, tiled=True)
        own_block = jnp.take(columns, own_ids, axis=0)
        own_diag = jnp.diagonal(own_block)
        gathered = lax.all_gather(own_diag, "row", axis=0, tiled=True)
        diag = gathered.reshape(groups, 2, half).transpose(1, 0, 2).reshape(width)
        inverse = 1.0 / jnp.sqrt(diag + eps_value)
        own_inverse = 1.0 / jnp.sqrt(own_diag + eps_value)
        normed = columns * inverse[:, None] * own_inverse[None, :]
        sign, positive, unit = sign_table(width, own_ids)
        local_sq = jnp.sum(jnp.where(positive, normed * normed, 0.0))
        total = lax.psum(local_sq, "row")
        scale = 1.0 / (1.0 + jnp.sqrt(total))
        iterate = unit + sign * normed * scale
        for step in range(NS_STEPS):
            current = iterate
            piece = lax.all_gather(current, "row", axis=1, tiled=True)
            folded = product(piece, product(piece.T, current))
            iterate = 1.5 * current - 0.5 * folded
        turned = product(work, lax.all_gather(iterate, "row", axis=1, tiled=True))
        work = turned.reshape(-1, groups, 2, half).transpose(0, 2, 1, 3).reshape(-1, width)
        second = from_behind(work[:, BLK:], "pair", 1)
        blocks = jnp.concatenate([work[:, :BLK], second], axis=1)
    return blocks


def solution(mesh):
    placed = (P("row", "pair"), P())
    return jax.shard_map(
        shards, mesh=mesh, in_specs=placed, out_specs=P("row", "pair"), check_vma=False
    )
```

profile of v0, /device:TPU:1, one launch (start us, length us, event | category | flops | bytes accessed | tf_op | source)
XLA Modules:
  0.0 1138.3 jit_solution(16740906257814945387)
XLA Ops:
  7.3 1.6 copy.18
  8.9 1.6 gather_fusion.2
  10.5 2.0 fusion.12
  15.7 109.5 %reduce-scatter.3.cloned.1.call-done = f32[512,32]{0,1:T(8,128)} async-done(((f32[512,512]{0,1:T(8,128)}), f32[512,32]{0,1:T(8,128)}) %reduce-scatter.3.cloned.1.call-update) | async-done | bytes 65552 | tf_op jit(solution)/shard_map/reduce_scatter | solution.py:48
  127.8 63.5 %all-reduce = f32[512]{0:T(512)S(1)} all-reduce(f32[512]{0:T(512)S(1)} %dynamic-update-slice), channel_id=1, replica_groups=mesh['pair'=32,'row'=16] {'row'}, use_global_device_ids=true, to_apply=%add | all-reduce | flops 512 | bytes 4096
  192.3 62.6 %psum.14 = f32[]{:T(128)} all-reduce(f32[]{:T(128)} %fusion.26), channel_id=1, replica_groups=mesh['pair'=32,'row'=16] {'row'}, use_global_device_ids=true, to_apply=%region_2.5 | all-reduce | flops 1 | bytes 8 | tf_op jit(solution)/shard_map/psum | solution.py:58
  256.4 76.3 %all-gather.9.cloned.1.call-done = f32[512,512]{0,1:T(8,128)} async-done(((f32[512,32]{0,1:T(8,128)}), f32[512,512]{0,1:T(8,128)}) %all-gather.9.cloned.1.call-update) | async-done | bytes 1048592 | tf_op jit(solution)/shard_map/all_gather | solution.py:63
  332.7 2.4 fusion.38
  335.1 1.4 fusion.5
  336.6 68.6 %all-gather.11.cloned.1.call-done = f32[512,512]{0,1:T(8,128)} async-done(((f32[512,32]{0,1:T(8,128)}), f32[512,512]{0,1:T(8,128)}) %all-gather.11.cloned.1.call-update) | async-done | bytes 1048592 | tf_op jit(solution)/shard_map/all_gather | solution.py:63
  405.2 2.4 fusion.39
  409.0 68.6 %all-gather.13.cloned.1.call-done = f32[512,512]{0,1:T(8,128)} async-done(((f32[512,32]{0,1:T(8,128)}), f32[512,512]{0,1:T(8,128)}) %all-gather.13.cloned.1.call-update) | async-done | bytes 1048592 | tf_op jit(solution)/shard_map/all_gather | solution.py:63
  477.6 2.4 fusion.40
  481.5 68.6 %all-gather.15.cloned.1.call-done = f32[512,512]{0,1:T(8,128)} async-done(((f32[512,32]{0,1:T(8,128)}), f32[512,512]{0,1:T(8,128)}) %all-gather.15.cloned.1.call-update) | async-done | bytes 1048592 | tf_op jit(solution)/shard_map/all_gather | solution.py:66
  550.1 3.2 fusion.10
  553.5 2.1 collective-permute-start
  555.6 21.7 %collective-permute-done = f32[512,256]{0,1:T(8,128)S(1)} collective-permute-done((f32[512,256]{0,1:T(8,128)S(1)}, f32[512,256]{0,1:T(8,128)S(1)}, u32[]{:S(2)}, u32[]{:S(2)}) %collective-permute-start) | collective-permute-done | bytes 524320 | tf_op jit(solution)/shard_map/ppermute | solution.py:14
  577.4 1.6 gather_fusion.4
  579.0 2.0 fusion.8
  582.1 95.9 %reduce-scatter.5.cloned.1.call-done = f32[512,32]{0,1:T(8,128)} async-done(((f32[512,512]{0,1:T(8,128)}), f32[512,32]{0,1:T(8,128)}) %reduce-scatter.5.cloned.1.call-update) | async-done | bytes 65552 | tf_op jit(solution)/shard_map/reduce_scatter | solution.py:48
  680.7 63.6 %all-reduce.1 = f32[512]{0:T(512)S(1)} all-reduce(f32[512]{0:T(512)S(1)} %dynamic-update-slice.1), channel_id=1, replica_groups=mesh['pair'=32,'row'=16] {'row'}, use_global_device_ids=true, to_apply=%add.1 | all-reduce | flops 512 | bytes 4096
  745.1 62.6 %psum.15 = f32[]{:T(128)} all-reduce(f32[]{:T(128)} %fusion.27), channel_id=1, replica_groups=mesh['pair'=32,'row'=16] {'row'}, use_global_device_ids=true, to_apply=%region_5.8 | all-reduce | flops 1 | bytes 8 | tf_op jit(solution)/shard_map/psum | solution.py:58
  809.3 76.3 %all-gather.17.cloned.1.call-done = f32[512,512]{0,1:T(8,128)} async-done(((f32[512,32]{0,1:T(8,128)}), f32[512,512]{0,1:T(8,128)}) %all-gather.17.cloned.1.call-update) | async-done | bytes 1048592 | tf_op jit(solution)/shard_map/all_gather | solution.py:63
  885.6 2.4 fusion.41
  889.4 68.6 %all-gather.19.cloned.1.call-done = f32[512,512]{0,1:T(8,128)} async-done(((f32[512,32]{0,1:T(8,128)}), f32[512,512]{0,1:T(8,128)}) %all-gather.19.cloned.1.call-update) | async-done | bytes 1048592 | tf_op jit(solution)/shard_map/all_gather | solution.py:63
  958.0 2.4 fusion.42
  961.8 68.6 %all-gather.21.cloned.1.call-done = f32[512,512]{0,1:T(8,128)} async-done(((f32[512,32]{0,1:T(8,128)}), f32[512,512]{0,1:T(8,128)}) %all-gather.21.cloned.1.call-update) | async-done | bytes 1048592 | tf_op jit(solution)/shard_map/all_gather | solution.py:63
  1030.5 2.4 fusion.43
  1034.2 68.7 %all-gather.23.cloned.1.call-done = f32[512,512]{0,1:T(8,128)} async-done(((f32[512,32]{0,1:T(8,128)}), f32[512,512]{0,1:T(8,128)}) %all-gather.23.cloned.1.call-update) | async-done | bytes 1048592 | tf_op jit(solution)/shard_map/all_gather | solution.py:66
  1102.9 3.2 fusion.6
  1106.3 1.9 collective-permute-start.1
  1108.2 21.9 %collective-permute-done.1 = f32[512,256]{0,1:T(8,128)S(1)} collective-permute-done((f32[512,256]{0,1:T(8,128)S(1)}, f32[512,256]{0,1:T(8,128)S(1)}, u32[]{:S(2)}, u32[]{:S(2)}) %collective-permute-start.1) | collective-permute-done | bytes 524320 | tf_op jit(solution)/shard_map/ppermute | solution.py:14
  (103 shorter events, 21.8 us)
Async XLA Ops:
  6.5 118.7 %reduce-scatter.3.cloned.1.call-start = ((), (), s32[]{:S(2)}) async-start(), calls=%async_computation.2 | async-start | bytes 1114112 | tf_op jit(solution)/shard_map/reduce_scatter | solution.py:48
  13.6 319.1 %all-gather.9.cloned.1.call-start = ((), (), s32[]{:S(2)}) async-start(), calls=%async_computation.3 | async-start | bytes 1114112 | tf_op jit(solution)/shard_map/all_gather | solution.py:63
  127.6 64.0 %copy-start.12 = (f32[512,32]{0,1:T(8,128)S(1)}, f32[512,32]{0,1:T(8,128)}, u32[]{:S(2)}) copy-start(f32[512,32]{0,1:T(8,128)} %reduce-scatter.3.cloned.1.call-done) | copy-start | bytes 196612
  256.3 76.4 %copy-start.11 = (f32[512,32]{0,1:T(8,128)S(1)}, f32[512,32]{0,1:T(8,128)}, u32[]{:S(2)}) copy-start(f32[512,32]{0,1:T(8,128)} %convert_add_fusion.1) | copy-start | bytes 196612
  256.4 148.8 %all-gather.11.cloned.1.call-start = ((), (), s32[]{:S(2)}) async-start(), calls=%async_computation.4 | async-start | bytes 1114112 | tf_op jit(solution)/shard_map/all_gather | solution.py:63
  332.7 2.4 copy-start
  336.5 68.7 %copy-start.6 = (f32[512,32]{0,1:T(8,128)S(1)}, f32[512,32]{0,1:T(8,128)}, u32[]{:S(2)}) copy-start(f32[512,32]{0,1:T(8,128)} %fusion.5) | copy-start | bytes 196612
  336.5 141.1 %all-gather.13.cloned.1.call-start = ((), (), s32[]{:S(2)}) async-start(), calls=%async_computation.5 | async-start | bytes 1114112 | tf_op jit(solution)/shard_map/all_gather | solution.py:63
  405.2 2.4 copy-start.1
  408.9 68.7 %copy-start.7 = (f32[512,32]{0,1:T(8,128)S(1)}, f32[512,32]{0,1:T(8,128)}, u32[]{:S(2)}) copy-start(f32[512,32]{0,1:T(8,128)} %fusion.4) | copy-start | bytes 196612
  409.0 141.1 %all-gather.15.cloned.1.call-start = ((), (), s32[]{:S(2)}) async-start(), calls=%async_computation.6 | async-start | bytes 1114112 | tf_op jit(solution)/shard_map/all_gather | solution.py:66
  477.6 2.4 copy-start.2
  481.4 196.7 %reduce-scatter.5.cloned.1.call-start = ((), (), s32[]{:S(2)}) async-start(), calls=%async_computation.7 | async-start | bytes 1114112 | tf_op jit(solution)/shard_map/reduce_scatter | solution.py:48
  553.5 23.8 %collective-permute-start = (f32[512,256]{0,1:T(8,128)S(1)}, f32[512,256]{0,1:T(8,128)S(1)}, u32[]{:S(2)}, u32[]{:S(2)}) collective-permute-start(f32[512,256]{0,1:T(8,128)S(1)} %get-tuple-element.10), channel_id=1, source_target_pairs={{0,16},{16,32},{32,48},{48,64},{64,80},{80,96},{96,112},{112,128},... | collective-permute-start | bytes 1572872 | tf_op jit(solution)/shard_map/ppermute | solution.py:14
  582.1 303.4 %all-gather.17.cloned.1.call-start = ((), (), s32[]{:S(2)}) async-start(), calls=%async_computation.8 | async-start | bytes 1114112 | tf_op jit(solution)/shard_map/all_gather | solution.py:63
  680.4 64.0 %copy-start.13 = (f32[512,32]{0,1:T(8,128)S(1)}, f32[512,32]{0,1:T(8,128)}, u32[]{:S(2)}) copy-start(f32[512,32]{0,1:T(8,128)} %reduce-scatter.5.cloned.1.call-done) | copy-start | bytes 196612
  809.2 76.4 %copy-start.10 = (f32[512,32]{0,1:T(8,128)S(1)}, f32[512,32]{0,1:T(8,128)}, u32[]{:S(2)}) copy-start(f32[512,32]{0,1:T(8,128)} %convert_add_fusion) | copy-start | bytes 196612
  809.2 148.8 %all-gather.19.cloned.1.call-start = ((), (), s32[]{:S(2)}) async-start(), calls=%async_computation.9 | async-start | bytes 1114112 | tf_op jit(solution)/shard_map/all_gather | solution.py:63
  885.6 2.4 copy-start.3
  889.3 68.7 %copy-start.8 = (f32[512,32]{0,1:T(8,128)S(1)}, f32[512,32]{0,1:T(8,128)}, u32[]{:S(2)}) copy-start(f32[512,32]{0,1:T(8,128)} %fusion.2) | copy-start | bytes 196612
  889.3 141.1 %all-gather.21.cloned.1.call-start = ((), (), s32[]{:S(2)}) async-start(), calls=%async_computation.10 | async-start | bytes 1114112 | tf_op jit(solution)/shard_map/all_gather | solution.py:63
  958.0 2.4 copy-start.4
  961.8 68.7 %copy-start.9 = (f32[512,32]{0,1:T(8,128)S(1)}, f32[512,32]{0,1:T(8,128)}, u32[]{:S(2)}) copy-start(f32[512,32]{0,1:T(8,128)} %fusion.1) | copy-start | bytes 196612
  961.8 141.1 %all-gather.23.cloned.1.call-start = ((), (), s32[]{:S(2)}) async-start(), calls=%async_computation.11 | async-start | bytes 1114112 | tf_op jit(solution)/shard_map/all_gather | solution.py:66
  1030.5 2.4 copy-start.5
  1106.3 23.8 %collective-permute-start.1 = (f32[512,256]{0,1:T(8,128)S(1)}, f32[512,256]{0,1:T(8,128)S(1)}, u32[]{:S(2)}, u32[]{:S(2)}) collective-permute-start(f32[512,256]{0,1:T(8,128)S(1)} %get-tuple-element.8), channel_id=1, source_target_pairs={{0,16},{16,32},{32,48},{48,64},{64,80},{80,96},{96,112},{112,128},... | collective-permute-start | bytes 1572872 | tf_op jit(solution)/shard_map/ppermute | solution.py:14
Sparse Core Ops, SparseCore 0:
  13.8 111.4 reduce-scatter.2
  256.5 76.1 all-gather.8
  336.6 68.5 all-gather.10
  409.1 68.4 all-gather.12
  481.5 68.4 all-gather.14
  582.2 95.7 reduce-scatter.4
  809.3 76.1 all-gather.16
  889.5 68.4 all-gather.18
  961.9 68.5 all-gather.20
  1034.3 68.4 all-gather.22
where the time goes:
time: 1140 us
  waiting for transfers between devices  813 us (71%)
  blocking collectives  252 us (22%)
  matrix products  32.9 us (3%)
  local copies, waits for them, and re-layouts  16 us (1%)
  between operations  16 us (1%)
    all_gather x6, waiting for transfers between devices, shards(): piece = lax.all_gather(current, 'row', axis=1, tiled=True)  427 us
    reduce_scatter x2, waiting for transfers between devices, shards(): columns = lax.psum_scatter(mixed, 'row', scatter_dimension=1, tiled=True)  205 us
    all_gather x2, waiting for transfers between devices, shards(): turned = product(work, lax.all_gather(iterate, 'row', axis=1, tiled=True))  137 us
    unnamed x2, blocking collectives  127 us
    psum x2, blocking collectives, shards(): total = lax.psum(local_sq, 'row')  125 us
    ppermute x2, waiting for transfers between devices, from_behind(): lax.ppermute(value, axis, [(i, (i + by) % devices) for i in range(devices)])  43.5 us
    dot_general x16, matrix products, product(): jnp.dot(left, right, precision=lax.Precision.HIGHEST, preferred_element_t...  32.9 us
  transfers between devices with their start and end apart: 12, of which 12 were waited for; matrix products, arithmetic and copies ran while one was open for 0% of the time, Pallas kernels for 0%

commit v1 on v0

--- a/solution.py
+++ b/solution.py
@@ -2,6 +2,7 @@
 import jax.numpy as jnp
 from jax import lax
 from jax.sharding import PartitionSpec as P
+from jax.lax import all_to_all, axis_size
 
 BLK = 256
 ROUNDS = 2
@@ -60,7 +61,10 @@
         iterate = unit + sign * normed * scale
         for step in range(NS_STEPS):
             current = iterate
-            piece = lax.all_gather(current, "row", axis=1, tiled=True)
+            heads_enter = lambda inputs, array_axis: jnp.concatenate(
+                all_to_all(jnp.stack(axis_size("row") * [inputs]), "row", 0, 0), axis=array_axis
+            )
+            piece = heads_enter(current, 1)
             folded = product(piece, product(piece.T, current))
             iterate = 1.5 * current - 0.5 * folded
         turned = product(work, lax.all_gather(iterate, "row", axis=1, tiled=True))

time: 1140 us -> 1030 us (0.904)
  waiting for transfers between devices: 813 us -> 394 us
  blocking collectives: 252 us -> 574 us
    all_gather x6 -> x0, waiting for transfers between devices: 427 us -> none  [shards(): piece = lax.all_gather(current, 'row', axis=1, tiled=True)]
    all_to_all x0 -> x6, blocking collectives: none -> 322 us  [shards(): all_to_all(jnp.stack(axis_size('row') * [inputs]), 'row', 0, 0)]
  transfers between devices with their start and end apart: 12 -> 6, of which waited for: 12 -> 6; matrix products, arithmetic and copies ran while one was open for 0% -> 0% of each run, Pallas kernels for 0% -> 0%
where the time goes in v1:
time: 1030 us
  blocking collectives  574 us (56%)
  waiting for transfers between devices  394 us (38%)
  matrix products  22.6 us (2%)
  local copies, waits for them, and re-layouts  16.6 us (2%)
  between operations  15.7 us (2%)
    all_to_all x6, blocking collectives, shards(): all_to_all(jnp.stack(axis_size('row') * [inputs]), 'row', 0, 0)  322 us
    reduce_scatter x2, waiting for transfers between devices, shards(): columns = lax.psum_scatter(mixed, 'row', scatter_dimension=1, tiled=True)  205 us
    all_gather x2, waiting for transfers between devices, shards(): turned = product(work, lax.all_gather(iterate, 'row', axis=1, tiled=True))  145 us
    unnamed x2, blocking collectives  127 us
    psum x2, blocking collectives, shards(): total = lax.psum(local_sq, 'row')  125 us
    ppermute x2, waiting for transfers between devices, from_behind(): lax.ppermute(value, axis, [(i, (i + by) % devices) for i in range(devices)])  43.5 us
    dot_general x16, matrix products, product(): jnp.dot(left, right, precision=lax.Precision.HIGHEST, preferred_element_t...  22.6 us
  transfers between devices with their start and end apart: 6, of which 6 were waited for; matrix products, arithmetic and copies ran while one was open for 0% of the time, Pallas kernels for 0%

profile of v1, /device:TPU:1, one launch (start us, length us, event | category | flops | bytes accessed | tf_op | source)
XLA Modules:
  0.0 1029.3 jit_solution(15536687301298049592)
XLA Ops:
  7.3 1.6 copy.24
  8.9 1.6 gather_fusion.2
  10.5 2.0 fusion.12
  13.7 1.3 dynamic-slice
  15.8 109.5 %reduce-scatter.3.cloned.1.call-done = f32[512,32]{0,1:T(8,128)} async-done(((f32[512,512]{0,1:T(8,128)}), f32[512,32]{0,1:T(8,128)}) %reduce-scatter.3.cloned.1.call-update) | async-done | bytes 65552 | tf_op jit(solution)/shard_map/reduce_scatter | solution.py:49
  127.9 63.5 %all-reduce = f32[512]{0:T(512)S(1)} all-reduce(f32[512]{0:T(512)S(1)} %dynamic-update-slice), channel_id=1, replica_groups=mesh['pair'=32,'row'=16] {'row'}, use_global_device_ids=true, to_apply=%add | all-reduce | flops 512 | bytes 4096
  192.3 62.6 %psum.14 = f32[]{:T(128)} all-reduce(f32[]{:T(128)} %fusion.26), channel_id=1, replica_groups=mesh['pair'=32,'row'=16] {'row'}, use_global_device_ids=true, to_apply=%region_2.5 | all-reduce | flops 1 | bytes 8 | tf_op jit(solution)/shard_map/psum | solution.py:59
  255.9 62.1 %all_to_all.30 = f32[16,512,32]{1,2,0:T(8,128)S(1)} all-to-all(f32[16,512,32]{1,2,0:T(8,128)S(1)} %stack.12), channel_id=1, replica_groups=mesh['pair'=32,'row'=16] {'row'}, dimensions={0} | all-to-all | bytes 2097152 | tf_op jit(solution)/shard_map/all_to_all | solution.py:65
  317.9 1.1 fusion.38
  319.9 51.6 %all_to_all.31 = f32[16,512,32]{1,2,0:T(8,128)S(1)} all-to-all(f32[16,512,32]{1,2,0:T(8,128)S(1)} %stack.13), channel_id=1, replica_groups=mesh['pair'=32,'row'=16] {'row'}, dimensions={0} | all-to-all | bytes 2097152 | tf_op jit(solution)/shard_map/all_to_all | solution.py:65
  373.4 47.4 %all_to_all.32 = f32[16,512,32]{1,2,0:T(8,128)S(1)} all-to-all(f32[16,512,32]{1,2,0:T(8,128)S(1)} %stack.14), channel_id=1, replica_groups=mesh['pair'=32,'row'=16] {'row'}, dimensions={0} | all-to-all | bytes 2097152 | tf_op jit(solution)/shard_map/all_to_all | solution.py:65
  421.9 1.4 fusion.3
  423.4 72.4 %all-gather.3.cloned.1.call-done = f32[512,512]{0,1:T(8,128)} async-done(((f32[512,32]{0,1:T(8,128)}), f32[512,512]{0,1:T(8,128)}) %all-gather.3.cloned.1.call-update) | async-done | bytes 1048592 | tf_op jit(solution)/shard_map/all_gather | solution.py:70
  495.7 3.2 fusion.10
  499.1 2.1 collective-permute-start
  501.3 21.7 %collective-permute-done = f32[512,256]{0,1:T(8,128)S(1)} collective-permute-done((f32[512,256]{0,1:T(8,128)S(1)}, f32[512,256]{0,1:T(8,128)S(1)}, u32[]{:S(2)}, u32[]{:S(2)}) %collective-permute-start) | collective-permute-done | bytes 524320 | tf_op jit(solution)/shard_map/ppermute | solution.py:15
  523.0 1.6 gather_fusion.4
  524.6 2.0 fusion.8
  527.8 96.0 %reduce-scatter.5.cloned.1.call-done = f32[512,32]{0,1:T(8,128)} async-done(((f32[512,512]{0,1:T(8,128)}), f32[512,32]{0,1:T(8,128)}) %reduce-scatter.5.cloned.1.call-update) | async-done | bytes 65552 | tf_op jit(solution)/shard_map/reduce_scatter | solution.py:49
  626.4 63.5 %all-reduce.1 = f32[512]{0:T(512)S(1)} all-reduce(f32[512]{0:T(512)S(1)} %dynamic-update-slice.1), channel_id=1, replica_groups=mesh['pair'=32,'row'=16] {'row'}, use_global_device_ids=true, to_apply=%add.1 | all-reduce | flops 512 | bytes 4096
  690.8 62.6 %psum.15 = f32[]{:T(128)} all-reduce(f32[]{:T(128)} %fusion.27), channel_id=1, replica_groups=mesh['pair'=32,'row'=16] {'row'}, use_global_device_ids=true, to_apply=%region_5.8 | all-reduce | flops 1 | bytes 8 | tf_op jit(solution)/shard_map/psum | solution.py:59
  754.4 62.0 %all_to_all.33 = f32[16,512,32]{1,2,0:T(8,128)S(1)} all-to-all(f32[16,512,32]{1,2,0:T(8,128)S(1)} %stack.15), channel_id=1, replica_groups=mesh['pair'=32,'row'=16] {'row'}, dimensions={0} | all-to-all | bytes 2097152 | tf_op jit(solution)/shard_map/all_to_all | solution.py:65
  816.4 1.1 fusion.41
  818.3 51.6 %all_to_all.34 = f32[16,512,32]{1,2,0:T(8,128)S(1)} all-to-all(f32[16,512,32]{1,2,0:T(8,128)S(1)} %stack.16), channel_id=1, replica_groups=mesh['pair'=32,'row'=16] {'row'}, dimensions={0} | all-to-all | bytes 2097152 | tf_op jit(solution)/shard_map/all_to_all | solution.py:65
  870.0 1.1 fusion.42
  871.9 47.5 %all_to_all.35 = f32[16,512,32]{1,2,0:T(8,128)S(1)} all-to-all(f32[16,512,32]{1,2,0:T(8,128)S(1)} %stack.17), channel_id=1, replica_groups=mesh['pair'=32,'row'=16] {'row'}, dimensions={0} | all-to-all | bytes 2097152 | tf_op jit(solution)/shard_map/all_to_all | solution.py:65
  920.4 1.4 fusion
  921.8 72.4 %all-gather.5.cloned.1.call-done = f32[512,512]{0,1:T(8,128)} async-done(((f32[512,32]{0,1:T(8,128)}), f32[512,512]{0,1:T(8,128)}) %all-gather.5.cloned.1.call-update) | async-done | bytes 1048592 | tf_op jit(solution)/shard_map/all_gather | solution.py:70
  994.2 3.2 fusion.6
  997.6 1.9 collective-permute-start.1
  999.5 21.9 %collective-permute-done.1 = f32[512,256]{0,1:T(8,128)S(1)} collective-permute-done((f32[512,256]{0,1:T(8,128)S(1)}, f32[512,256]{0,1:T(8,128)S(1)}, u32[]{:S(2)}, u32[]{:S(2)}) %collective-permute-start.1) | collective-permute-done | bytes 524320 | tf_op jit(solution)/shard_map/ppermute | solution.py:15
  1021.5 1.3 copy.33
  (73 shorter events, 17.5 us)
Async XLA Ops:
  6.5 118.8 %reduce-scatter.3.cloned.1.call-start = ((), (), s32[]{:S(2)}) async-start(), calls=%async_computation.8 | async-start | bytes 1114112 | tf_op jit(solution)/shard_map/reduce_scatter | solution.py:49
  13.6 482.1 %all-gather.3.cloned.1.call-start = ((), (), s32[]{:S(2)}) async-start(), calls=%async_computation.9 | async-start | bytes 1114112 | tf_op jit(solution)/shard_map/all_gather | solution.py:70
  127.7 63.9 %copy-start = (f32[512,32]{0,1:T(8,128)S(1)}, f32[512,32]{0,1:T(8,128)}, u32[]{:S(2)}) copy-start(f32[512,32]{0,1:T(8,128)} %reduce-scatter.3.cloned.1.call-done) | copy-start | bytes 196612
  423.3 200.5 %reduce-scatter.5.cloned.1.call-start = ((), (), s32[]{:S(2)}) async-start(), calls=%async_computation.10 | async-start | bytes 1114112 | tf_op jit(solution)/shard_map/reduce_scatter | solution.py:49
  499.1 23.8 %collective-permute-start = (f32[512,256]{0,1:T(8,128)S(1)}, f32[512,256]{0,1:T(8,128)S(1)}, u32[]{:S(2)}, u32[]{:S(2)}) collective-permute-start(f32[512,256]{0,1:T(8,128)S(1)} %get-tuple-element.10), channel_id=1, source_target_pairs={{0,16},{16,32},{32,48},{48,64},{64,80},{80,96},{96,112},{112,128},... | collective-permute-start | bytes 1572872 | tf_op jit(solution)/shard_map/ppermute | solution.py:15
  527.8 466.4 %all-gather.5.cloned.1.call-start = ((), (), s32[]{:S(2)}) async-start(), calls=%async_computation.11 | async-start | bytes 1114112 | tf_op jit(solution)/shard_map/all_gather | solution.py:70
  626.1 63.9 %copy-start.1 = (f32[512,32]{0,1:T(8,128)S(1)}, f32[512,32]{0,1:T(8,128)}, u32[]{:S(2)}) copy-start(f32[512,32]{0,1:T(8,128)} %reduce-scatter.5.cloned.1.call-done) | copy-start | bytes 196612
  997.6 23.8 %collective-permute-start.1 = (f32[512,256]{0,1:T(8,128)S(1)}, f32[512,256]{0,1:T(8,128)S(1)}, u32[]{:S(2)}, u32[]{:S(2)}) collective-permute-start(f32[512,256]{0,1:T(8,128)S(1)} %get-tuple-element.8), channel_id=1, source_target_pairs={{0,16},{16,32},{32,48},{48,64},{64,80},{80,96},{96,112},{112,128},... | collective-permute-start | bytes 1572872 | tf_op jit(solution)/shard_map/ppermute | solution.py:15
Sparse Core Ops, SparseCore 0:
  13.8 111.5 reduce-scatter.2
  423.4 72.2 all-gather.2
  527.9 95.8 reduce-scatter.4
  921.9 72.1 all-gather.4
